TPU v7x, 32 devices: a whole 2x2x4 slice. The times are simulated.
32 devices in a mesh: groups: 2 (over x), tm: 16 (over z, y, core).
Axes of the slice: x: 2, y: 2, z: 4, core: 2. Of those that a mesh axis runs over, the one named last changes fastest.
Arguments:
- samples: float32 [16384, 2048], P('groups', 'tm'), parts along dimension 0, may hold values from -6 to 6
- test_matrix: float32 [4096, 256], P(('groups', 'tm')), parts along dimension 0, may hold values from -0.125 to 0.125
Outputs:
- basis: float32 [16384, 256], P(('groups', 'tm')), parts along dimension 0
- coordinates: float32 [512, 2048], P('groups', 'tm'), parts along dimension 0
There are 2 independent parts, one for each index of `groups`. A program takes and returns all parts, laid end to end along the dimension named above; each array names one. Nothing has to cross between parts.
All inputs are finite; a program needn't handle non-finite values.
Results may differ from a plain program's by a relative error of at most 0.0003.
Values sent between devices are 32-bit elements; how exact they have to be, the bound alone decides.
No kernel may reach another device: no remote copies, remote signals or barrier semaphores. Data moves between devices by JAX's collectives and lax.ppermute only.
A program may use at most 64 MiB of HBM per device.

v0:
```python
import jax
import jax.numpy as jnp
from jax import lax
from jax.sharding import PartitionSpec as P


def local_gram(rows):
    return jnp.dot(
        rows.T, rows, precision=lax.Precision.HIGHEST, preferred_element_type=jnp.float32
    )


def local(samples, test_matrix):
    highest = lax.Precision.HIGHEST
    channels = samples.shape[0]
    sample_rows = samples
    sketch = lax.psum_scatter(
        jnp.dot(sample_rows, test_matrix, precision=highest, preferred_element_type=jnp.float32),
        "tm",
        scatter_dimension=0,
        tiled=True,
    )
    sample_rows = samples
    projected = jnp.einsum(
        "rk,rs->ks",
        lax.all_gather(sketch, "tm", axis=0, tiled=True),
        sample_rows,
        precision=highest,
    )
    gram_one = lax.psum(local_gram(sketch), "tm")
    factor_one = jnp.linalg.cholesky(gram_one)
    orthonormal = jax.scipy.linalg.solve_triangular(factor_one, sketch.T, lower=True).T
    coordinates = jax.scipy.linalg.solve_triangular(factor_one, projected, lower=True)
    return (orthonormal * float(channels) ** 0.5, coordinates)


def solution(mesh):
    placed = (P("groups", "tm"), P(("groups", "tm"), None))
    return jax.shard_map(
        local,
        mesh=mesh,
        in_specs=placed,
        out_specs=(P(("groups", "tm"), None), P("groups", "tm")),
        check_vma=False,
    )
```

profile of v0, /device:TPU:0, one launch (start us, length us, event | category | flops | bytes accessed | tf_op | source)
XLA Modules:
  0.0 319.4 jit_solution(12343590044157621184)
XLA Ops:
  7.2 0.0 copy-start
  7.2 0.0 reduce-scatter.2.cloned.1.call-start
  7.2 0.8 copy-done
  8.1 10.4 %fusion.14 = f32[8192,256]{1,0:T(8,128)} fusion(f32[8192,128]{1,0:T(8,128)} %param.2, f32[128,256]{1,0:T(8,128)S(1)} %copy-done), kind=kOutput, calls=%fused_computation.36 | convolution fusion | flops 3221225472 | bytes 12713984 | tf_op jit(solution)/shard_map/dot_general | solution.py:18
  18.5 0.0 reduce-scatter.2.cloned.1.call-update
  18.5 0.0 all-reduce.3.cloned.1.call-start
  18.5 106.3 %reduce-scatter.2.cloned.1.call-done = f32[512,256]{1,0:T(8,128)} async-done(((f32[8192,256]{1,0:T(8,128)}), f32[512,256]{1,0:T(8,128)}) %reduce-scatter.2.cloned.1.call-update) | async-done | bytes 524304 | tf_op jit(solution)/shard_map/reduce_scatter | solution.py:17
  124.8 0.0 copy-start.1
  124.8 3.0 fusion.15
  127.8 0.0 all-reduce.3.cloned.1.call-update
  127.8 0.2 all-gather.2.cloned.1.call-start
  128.0 0.5 all-gather.2.cloned.1.call-update
  128.6 89.7 %all-reduce.3.cloned.1.call-done = f32[256,256]{0,1:T(8,128)} async-done(((f32[256,256]{0,1:T(8,128)}), f32[256,256]{0,1:T(8,128)}) %all-reduce.3.cloned.1.call-update) | async-done | bytes 262160 | tf_op jit(solution)/shard_map/psum | solution.py:30
  218.2 1.1 copy.5
  219.3 1.0 fusion.3
  220.3 11.7 %cholesky.50 = f32[128,128]{1,0:T(8,128)S(1)} custom-call(f32[128,128]{1,0:T(8,128)S(1)} %cholesky.118), custom_call_target="Cholesky" | custom-call | tf_op jit(solution)/shard_map/jit(cholesky)/cholesky | solution.py:31
  232.1 9.8 %custom-call.18 = f32[1,128,128]{1,2,0:T(8,128)S(1)} custom-call(f32[1,128,128]{2,1,0:T(8,128)S(1)} %get-tuple-element.25), custom_call_target="InvertDiagBlocksLowerTriangular" | custom-call | tf_op jit(solution)/shard_map/jit(cholesky)/cholesky | solution.py:31
  241.9 0.2 constant_dynamic-update-slice_fusion.1
  242.1 0.3 convolution_subtract_fusion.2
  242.4 11.7 %cholesky.105 = f32[128,128]{1,0:T(8,128)S(1)} custom-call(f32[128,128]{1,0:T(8,128)S(1)} %convolution_subtract_fusion.2), custom_call_target="Cholesky" | custom-call | tf_op jit(solution)/shard_map/jit(cholesky)/cholesky | solution.py:31
  254.1 0.7 compare_reduce_fusion
  256.1 0.1 triangular_solve.72
  256.2 4.1 %while.1 = (s32[]{:T(128)}, f32[256,256]{1,0:T(8,128)S(1)}, s32[2,2]{1,0:T(2,128)S(1)}, f32[2,128,128]{2,1,0:T(8,128)S(1)}, s32[]{:T(128)}) while((s32[]{:T(128)}, f32[256,256]{1,0:T(8,128)S(1)}, s32[2,2]{1,0:T(2,128)S(1)}, f32[2,128,128]{2,1,0:T(8,128)S(1)}, s32[]{:T(128)}) %tuple.28), condition=%wide.while_cond, body=%wide.while_body.sunk | while | flops 2 | bytes 131189 | solution.py:32
  256.4 0.6 fusion.30
  257.0 1.4 bitcast_dynamic-update-slice_fusion.2
  258.4 0.6 fusion.30
  259.0 1.4 bitcast_dynamic-update-slice_fusion.2
  260.4 19.7 %custom-call.19 = f32[2,128,128]{1,2,0:T(8,128)S(1)} custom-call(f32[2,128,128]{2,1,0:T(8,128)S(1)} %get-tuple-element.9), custom_call_target="InvertDiagBlocksLowerTriangular" | custom-call | tf_op jit(solution)/shard_map/jit(_solve_triangular)/triangular_solve | solution.py:32
  280.0 0.0 copy-done.1
  280.1 0.4 fusion.1
  280.5 0.6 convolution_subtract_fusion
  281.1 0.4 fusion.10
  281.5 0.1 fusion
  281.6 1.0 copy.6
  282.6 12.7 %all-gather.2.cloned.1.call-done = f32[8192,256]{1,0:T(8,128)} async-done(((f32[512,256]{1,0:T(8,128)}), f32[8192,256]{1,0:T(8,128)}) %all-gather.2.cloned.1.call-update) | async-done | bytes 8388624 | tf_op jit(solution)/shard_map/all_gather | solution.py:26
  295.2 16.2 %fusion.16 = f32[256,128]{1,0:T(8,128)S(1)} fusion(f32[8192,256]{1,0:T(8,128)} %all-gather.2.cloned.1.call-done, f32[8192,128]{1,0:T(8,128)} %param.2), kind=kOutput, calls=%fused_computation.38 | convolution fusion | flops 3221225472 | bytes 12713984 | tf_op jit(solution)/shard_map/rk,rs->ks/dot_general | solution.py:24
  311.5 0.3 fusion.4
  311.7 0.2 convolution_subtract_fusion.1
  312.0 0.3 fusion.9
  312.2 0.7 pad_maximum_fusion
  (9 shorter events, 0.1 us)
Async XLA Ops:
  7.2 0.9 copy-start
  7.2 117.6 %reduce-scatter.2.cloned.1.call-start = ((), (), s32[]{:S(2)}) async-start(), calls=%async_computation.1 | async-start | bytes 8912896 | tf_op jit(solution)/shard_map/reduce_scatter | solution.py:17
  18.5 199.7 %all-reduce.3.cloned.1.call-start = ((), (), s32[]{:S(2)}) async-start(), calls=%async_computation.2 | async-start | bytes 524288 | tf_op jit(solution)/shard_map/psum | solution.py:30
  124.8 155.2 %copy-start.1 = (f32[512,256]{1,0:T(8,128)S(1)}, f32[512,256]{1,0:T(8,128)}, u32[]{:S(2)}) copy-start(f32[512,256]{1,0:T(8,128)} %reduce-scatter.2.cloned.1.call-done) | copy-start | bytes 1572868
  127.8 167.4 %all-gather.2.cloned.1.call-start = ((), (), s32[]{:S(2)}) async-start(), calls=%async_computation.3 | async-start | bytes 8912896 | tf_op jit(solution)/shard_map/all_gather | solution.py:26
Sparse Core Ops, SparseCore 0:
  18.6 106.1 reduce-scatter.1
  128.8 89.3 all-reduce.2
  220.4 74.7 all-gather.1
where the time goes:
time: 320 us; the launch traced here: 319 us
  waiting for transfers between devices  209 us (65%)
  other arithmetic  55.4 us (17%)
  matrix products  32.2 us (10%)
  between operations  15.2 us (5%)
  local copies, waits for them, and re-layouts  6.96 us (2%)
    reduce_scatter x1, waiting for transfers between devices, local(): lax.psum_scatter(jnp.dot(sample_rows, test_matrix, precision=highest, pre...  106 us
    psum x1, waiting for transfers between devices, local(): gram_one = lax.psum(local_gram(sketch), 'tm')  89.7 us
    another operation x6, other arithmetic, local(): factor_one = jnp.linalg.cholesky(gram_one)  34 us
    another operation x3, other arithmetic, local(): jax.scipy.linalg.solve_triangular(factor_one, sketch.T, lower=True)  19.7 us
    dot_general x1, matrix products, local(): jnp.einsum('rk,rs->ks', lax.all_gather(sketch, 'tm', axis=0, tiled=True),...  16.2 us
    all_gather x1, waiting for transfers between devices, local(): lax.all_gather(sketch, 'tm', axis=0, tiled=True)  12.7 us
    dot_general x1, matrix products, local(): jnp.dot(sample_rows, test_matrix, precision=highest, preferred_element_ty...  10.4 us
  transfers between devices with their start and end apart: 3, of which 3 were waited for; matrix products, arithmetic and copies ran while one was open for 20% of the time, Pallas kernels for 0%

commit v1 on v0

--- a/solution.py
+++ b/solution.py
@@ -27,7 +27,9 @@
         sample_rows,
         precision=highest,
     )
-    gram_one = lax.psum(local_gram(sketch), "tm")
+    part = local_gram(sketch)
+    parts = lax.all_gather(part, "tm")
+    gram_one = jnp.sum(parts, axis=0)
     factor_one = jnp.linalg.cholesky(gram_one)
     orthonormal = jax.scipy.linalg.solve_triangular(factor_one, sketch.T, lower=True).T
     coordinates = jax.scipy.linalg.solve_triangular(factor_one, projected, lower=True)

time: 320 us -> 278 us (0.87)
  waiting for transfers between devices: 209 us -> 167 us
    psum x1 -> x0, waiting for transfers between devices: 89.7 us -> none  [local(): gram_one = lax.psum(local_gram(sketch), 'tm')]
    all_gather x0 -> x1, waiting for transfers between devices: none -> 49.4 us  [local(): parts = lax.all_gather(part, 'tm')]
  transfers between devices with their start and end apart: 3 -> 3, of which waited for: 3 -> 3; matrix products, arithmetic and copies ran while one was open for 20% -> 23% of each run, Pallas kernels for 0% -> 0%
where the time goes in v1:
time: 278 us
  waiting for transfers between devices  167 us (60%)
  other arithmetic  56.9 us (20%)
  matrix products  32.2 us (12%)
  between operations  15.1 us (5%)
  local copies, waits for them, and re-layouts  5.88 us (2%)
    reduce_scatter x1, waiting for transfers between devices, local(): lax.psum_scatter(jnp.dot(sample_rows, test_matrix, precision=highest, pre...  106 us
    all_gather x1, waiting for transfers between devices, local(): parts = lax.all_gather(part, 'tm')  49.4 us
    another operation x6, other arithmetic, local(): factor_one = jnp.linalg.cholesky(gram_one)  33.9 us
    another operation x3, other arithmetic, local(): jax.scipy.linalg.solve_triangular(factor_one, sketch.T, lower=True)  19.7 us
    dot_general x1, matrix products, local(): jnp.einsum('rk,rs->ks', lax.all_gather(sketch, 'tm', axis=0, tiled=True),...  16.2 us
    all_gather x1, waiting for transfers between devices, local(): lax.all_gather(sketch, 'tm', axis=0, tiled=True)  10.9 us
    dot_general x1, matrix products, local(): jnp.dot(sample_rows, test_matrix, precision=highest, preferred_element_ty...  10.4 us
  transfers between devices with their start and end apart: 3, of which 3 were waited for; matrix products, arithmetic and copies ran while one was open for 23% of the time, Pallas kernels for 0%

profile of v1, /device:TPU:0, one launch (start us, length us, event | category | flops | bytes accessed | tf_op | source)
XLA Modules:
  0.0 277.8 jit_solution(17123176891854260317)
XLA Ops:
  7.2 0.0 copy-start
  7.2 0.0 reduce-scatter.2.cloned.1.call-start
  7.2 0.8 copy-done
  8.1 10.4 %fusion.14 = f32[8192,256]{1,0:T(8,128)} fusion(f32[8192,128]{1,0:T(8,128)} %param.2, f32[128,256]{1,0:T(8,128)S(1)} %copy-done), kind=kOutput, calls=%fused_computation.36 | convolution fusion | flops 3221225472 | bytes 12713984 | tf_op jit(solution)/shard_map/dot_general | solution.py:18
  18.5 0.0 reduce-scatter.2.cloned.1.call-update
  18.5 0.0 all-gather.6.cloned.1.call-start
  18.5 106.3 %reduce-scatter.2.cloned.1.call-done = f32[512,256]{1,0:T(8,128)} async-done(((f32[8192,256]{1,0:T(8,128)}), f32[512,256]{1,0:T(8,128)}) %reduce-scatter.2.cloned.1.call-update) | async-done | bytes 524304 | tf_op jit(solution)/shard_map/reduce_scatter | solution.py:17
  124.8 2.9 %fusion.15 = f32[256,256]{1,0:T(8,128)} fusion(f32[512,256]{1,0:T(8,128)} %reduce-scatter.2.cloned.1.call-done), kind=kOutput, calls=%fused_computation.37 | convolution fusion | flops 402653184 | bytes 786432 | tf_op jit(solution)/shard_map/dot_general | solution.py:8
  127.7 0.0 all-gather.6.cloned.1.call-update
  127.8 0.2 all-gather.4.cloned.1.call-start
  128.0 0.5 all-gather.4.cloned.1.call-update
  128.5 49.4 %all-gather.6.cloned.1.call-done = f32[4096,256]{1,0:T(8,128)} async-done(((f32[256,256]{1,0:T(8,128)}), f32[4096,256]{1,0:T(8,128)}) %all-gather.6.cloned.1.call-update) | async-done | bytes 4194320 | tf_op jit(solution)/shard_map/all_gather | solution.py:31
  178.0 0.0 copy-start.1
  178.0 2.5 reduce_sum.9
  180.5 0.1 copy.6
  180.7 11.7 %cholesky.50 = f32[128,128]{1,0:T(8,128)S(1)} custom-call(f32[128,128]{1,0:T(8,128)S(1)} %cholesky.118), custom_call_target="Cholesky" | custom-call | tf_op jit(solution)/shard_map/jit(cholesky)/cholesky | solution.py:33
  192.5 9.8 %custom-call.18 = f32[1,128,128]{1,2,0:T(8,128)S(1)} custom-call(f32[1,128,128]{2,1,0:T(8,128)S(1)} %get-tuple-element.27), custom_call_target="InvertDiagBlocksLowerTriangular" | custom-call | tf_op jit(solution)/shard_map/jit(cholesky)/cholesky | solution.py:33
  202.3 0.2 constant_dynamic-update-slice_fusion.1
  202.5 0.3 convolution_subtract_fusion.2
  202.8 11.7 %cholesky.105 = f32[128,128]{1,0:T(8,128)S(1)} custom-call(f32[128,128]{1,0:T(8,128)S(1)} %convolution_subtract_fusion.2), custom_call_target="Cholesky" | custom-call | tf_op jit(solution)/shard_map/jit(cholesky)/cholesky | solution.py:33
  214.5 0.6 compare_reduce_fusion
  216.4 0.1 triangular_solve.72
  216.5 4.0 %while.1 = (s32[]{:T(128)}, f32[256,256]{1,0:T(8,128)S(1)}, s32[2,2]{1,0:T(2,128)S(1)}, f32[2,128,128]{2,1,0:T(8,128)S(1)}, s32[]{:T(128)}) while((s32[]{:T(128)}, f32[256,256]{1,0:T(8,128)S(1)}, s32[2,2]{1,0:T(2,128)S(1)}, f32[2,128,128]{2,1,0:T(8,128)S(1)}, s32[]{:T(128)}) %tuple.29), condition=%wide.while_cond, body=%wide.while_body.sunk | while | flops 2 | bytes 131189 | solution.py:34
  216.7 0.6 fusion.30
  217.2 1.3 bitcast_dynamic-update-slice_fusion.2
  218.6 0.6 fusion.30
  219.2 1.3 bitcast_dynamic-update-slice_fusion.2
  220.5 19.7 %custom-call.19 = f32[2,128,128]{1,2,0:T(8,128)S(1)} custom-call(f32[2,128,128]{2,1,0:T(8,128)S(1)} %get-tuple-element.9), custom_call_target="InvertDiagBlocksLowerTriangular" | custom-call | tf_op jit(solution)/shard_map/jit(_solve_triangular)/triangular_solve | solution.py:34
  240.2 0.0 copy-done.1
  240.2 0.4 fusion.1
  240.6 0.6 convolution_subtract_fusion
  241.2 0.4 fusion.10
  241.6 0.1 fusion
  241.7 1.0 copy.7
  242.7 10.9 %all-gather.4.cloned.1.call-done = f32[8192,256]{1,0:T(8,128)} async-done(((f32[512,256]{1,0:T(8,128)}), f32[8192,256]{1,0:T(8,128)}) %all-gather.4.cloned.1.call-update) | async-done | bytes 8388624 | tf_op jit(solution)/shard_map/all_gather | solution.py:26
  253.6 16.2 %fusion.16 = f32[256,128]{1,0:T(8,128)S(1)} fusion(f32[8192,256]{1,0:T(8,128)} %all-gather.4.cloned.1.call-done, f32[8192,128]{1,0:T(8,128)} %param.2), kind=kOutput, calls=%fused_computation.38 | convolution fusion | flops 3221225472 | bytes 12713984 | tf_op jit(solution)/shard_map/rk,rs->ks/dot_general | solution.py:24
  269.8 0.3 fusion.4
  270.1 0.2 convolution_subtract_fusion.1
  270.3 0.3 fusion.9
  270.6 0.7 pad_maximum_fusion
  (10 shorter events, 0.2 us)
Async XLA Ops:
  7.2 0.9 copy-start
  7.2 117.6 %reduce-scatter.2.cloned.1.call-start = ((), (), s32[]{:S(2)}) async-start(), calls=%async_computation.1 | async-start | bytes 8912896 | tf_op jit(solution)/shard_map/reduce_scatter | solution.py:17
  18.5 159.5 %all-gather.6.cloned.1.call-start = ((), (), s32[]{:S(2)}) async-start(), calls=%async_computation.3 | async-start | bytes 4456448 | tf_op jit(solution)/shard_map/all_gather | solution.py:31
  127.8 125.8 %all-gather.4.cloned.1.call-start = ((), (), s32[]{:S(2)}) async-start(), calls=%async_computation.2 | async-start | bytes 8912896 | tf_op jit(solution)/shard_map/all_gather | solution.py:26
  178.0 62.2 %copy-start.1 = (f32[512,256]{1,0:T(8,128)S(1)}, f32[512,256]{1,0:T(8,128)}, u32[]{:S(2)}) copy-start(f32[512,256]{1,0:T(8,128)} %reduce-scatter.2.cloned.1.call-done) | copy-start | bytes 1572868
Sparse Core Ops, SparseCore 0:
  18.6 106.1 reduce-scatter.1
  127.9 50.0 all-gather.5
  180.1 73.3 all-gather.3
